TPU v7x, 256 devices: a whole 4x4x8 slice. The times are simulated.
256 devices in a mesh: dp: 4 (over z_lo, core), ang: 4 (over y), rows: 16 (over z_hi, x).
Axes of the slice: x: 4, y: 4, z: 8 (z_hi: 4, z_lo: 2; z = z_hi * 2 + z_lo), core: 2. Of those that a mesh axis runs over, the one named last changes fastest.
Arguments:
- light_field: bfloat16 [4, 1, 8, 64, 64, 512], P('dp', None, 'ang', 'rows'), may hold values from -6 to 6
- spatial_weight: bfloat16 [3, 3, 64, 64], replicated, may hold values from -0.25 to 0.25
- epi_weight: bfloat16 [3, 3, 64, 64], replicated, may hold values from -0.25 to 0.25
- upsample_weight: bfloat16 [16, 64], replicated, may hold values from -0.75 to 0.75
- image_grad: bfloat16 [4, 1, 8, 256, 2048], P('dp', None, 'ang', 'rows'), may hold values from -0.005859375 to 0.005859375
Outputs:
- upscaled: bfloat16 [4, 1, 8, 256, 2048], P('dp', None, 'ang', 'rows')
- spatial_grad: float32 [3, 3, 64, 64], replicated
- epi_grad: float32 [3, 3, 64, 64], replicated
- upsample_grad: float32 [16, 64], replicated
All inputs are finite; a program needn't handle non-finite values.
Results may differ from a plain program's by a relative error of at most 0.0066.
Values may be sent and summed in bfloat16 or wider, within the bound.
No kernel may reach another device: no remote copies, remote signals or barrier semaphores. Data moves between devices by JAX's collectives and lax.ppermute only.
A program may use at most 64 MiB of HBM per device.

v0:
```python
import jax
import jax.numpy as jnp
from jax import lax
from jax.sharding import PartitionSpec as P

SCALE = 4
SUB = 16


def with_halo(cells, sides, width):
    for axis, dim in sides:
        count = lax.axis_size(axis)
        ends = count - 1
        head = lax.slice_in_dim(cells, 0, width, axis=dim)
        tail = lax.slice_in_dim(cells, cells.shape[dim] - width, cells.shape[dim], axis=dim)
        cells = jnp.concatenate(
            [
                lax.ppermute(tail, axis, [(i, (i + 1) % count) for i in range(ends)]),
                cells,
                lax.ppermute(head, axis, [((i + 1) % count, i) for i in range(ends)]),
            ],
            axis=dim,
        )
    return cells


def silu_slope(values):
    sigmoid_value = jax.nn.sigmoid(values)
    return sigmoid_value * (1.0 + values * (1.0 - sigmoid_value))


def spatial_conv(padded, weight, height, breadth):
    summed = jnp.zeros(padded.shape[:3] + (height, weight.shape[2], breadth), jnp.float32)
    for tap_row in range(3):
        for tap_col in range(3):
            summed = summed + jnp.einsum(
                "oc,buvhcw->buvhow",
                weight[tap_row, tap_col],
                padded[:, :, :, tap_row : tap_row + height, :, tap_col : tap_col + breadth],
                preferred_element_type=jnp.float32,
            )
    return summed


def epi_conv(padded, weight, views_all, breadth):
    summed = jnp.zeros(
        padded.shape[:2] + (views_all, padded.shape[3], weight.shape[2], breadth), jnp.float32
    )
    for tap_row in range(3):
        for tap_col in range(3):
            summed = summed + jnp.einsum(
                "oc,buvhcw->buvhow",
                weight[tap_row, tap_col],
                padded[:, :, tap_row : tap_row + views_all, :, :, tap_col : tap_col + breadth],
                preferred_element_type=jnp.float32,
            )
    return summed


def epi_back(padded, weight, views_all, breadth):
    summed = jnp.zeros(
        padded.shape[:2] + (views_all, padded.shape[3], weight.shape[3], breadth), jnp.float32
    )
    for tap_row in range(3):
        for tap_col in range(3):
            summed = summed + jnp.einsum(
                "oc,buvhow->buvhcw",
                weight[tap_row, tap_col],
                padded[
                    :,
                    :,
                    2 - tap_row : 2 - tap_row + views_all,
                    :,
                    :,
                    2 - tap_col : 2 - tap_col + breadth,
                ],
                preferred_element_type=jnp.float32,
            )
    return summed


def weight_grad(upstream, padded, along_dim, extent, breadth):
    rows_out = []
    for tap_row in range(3):
        row_list = []
        for tap_col in range(3):
            window = lax.slice_in_dim(padded, tap_row, tap_row + extent, axis=along_dim)
            window = lax.slice_in_dim(window, tap_col, tap_col + breadth, axis=5)
            row_list.append(
                jnp.einsum(
                    "buvhow,buvhcw->oc", upstream, window, preferred_element_type=jnp.float32
                )
            )
        rows_out.append(jnp.stack(row_list))
    return jnp.stack(rows_out)


def project_up(weight, features):
    return jnp.einsum(
        "sc,buvhcw->buvhsw", weight, features, preferred_element_type=jnp.float32
    ).astype(jnp.bfloat16)


def shift_pairs(kind, step):
    if kind == "x":
        return ("rows", [(g * 4 + i, g * 4 + (i + step) % 4) for g in range(4) for i in range(4)])
    if kind == "z":
        return ("rows", [(4 * i + g, 4 * ((i + step) % 4) + g) for g in range(4) for i in range(4)])
    return (kind, [(i, (i + step) % 4) for i in range(4)])


def place_in(kind):
    if kind == "x":
        return lax.axis_index("rows") % 4
    if kind == "z":
        return lax.axis_index("rows") // 4
    return lax.axis_index(kind)


def shifted(value, kind, step):
    axis, pairs = shift_pairs(kind, step)
    return lax.ppermute(value, axis, pairs)


def gather_sum(value, kind):
    one, two, three = (shifted(value, kind, step) for step in (1, 2, 3))
    return value + two + (one + three)


def scatter_sum(value, kind):
    place = place_in(kind)
    mine = lax.dynamic_index_in_dim(value, place, 0, keepdims=False)
    one, two, three = (
        shifted(lax.dynamic_index_in_dim(value, (place + step) % 4, 0, keepdims=False), kind, step)
        for step in (1, 2, 3)
    )
    return mine + two + (one + three)


def gather_parts(value, kind):
    place = place_in(kind)
    around = jnp.stack([value] + [shifted(value, kind, step) for step in (1, 2, 3)])
    return jnp.concatenate(
        [lax.dynamic_index_in_dim(around, (place - part) % 4, 0) for part in range(4)], axis=0
    )


def sum_everywhere(parts):
    flat = jnp.concatenate([part.reshape(-1, 128) for part in parts], axis=0)
    rows = flat.shape[0]
    share = -(-rows // 32) * 8
    flat = jnp.pad(flat, ((0, 4 * share - rows), (0, 0))).reshape(4, share, 128)
    mine = scatter_sum(flat, "dp")
    for kind in ("x", "z", "ang"):
        mine = gather_sum(mine, kind)
    flat = gather_parts(mine, "dp").reshape(4 * share, 128)
    results, start = ([], 0)
    for part in parts:
        count = part.size // 128
        results.append(flat[start : start + count].reshape(part.shape))
        start += count
    return results


def on_device(light_field, spatial_weight, epi_weight, upsample_weight, image_grad):
    batch_here, angular_rows, views_here, rows_here, channels, breadth = light_field.shape
    rimmed = with_halo(light_field, (("rows", 3),), 1)
    spatial_in = jnp.pad(rimmed, ((0, 0), (0, 0), (0, 0), (0, 0), (0, 0), (1, 1)))
    spatial_out = spatial_conv(spatial_in, spatial_weight, rows_here, breadth)
    first = (light_field.astype(jnp.float32) + jax.nn.silu(spatial_out)).astype(jnp.bfloat16)
    cotangent = image_grad.reshape(
        batch_here, angular_rows, views_here, rows_here, SCALE, breadth, SCALE
    )
    cotangent = cotangent.transpose(0, 1, 2, 3, 4, 6, 5).reshape(
        batch_here, angular_rows, views_here, rows_here, SUB, breadth
    )
    epi_block = lax.all_to_all(first, "ang", split_axis=3, concat_axis=2, tiled=True)
    views_block = epi_block.shape[2]
    padded_block = jnp.pad(epi_block, ((0, 0), (0, 0), (1, 1), (0, 0), (0, 0), (1, 1)))
    block_out = epi_conv(padded_block, epi_weight, views_block, breadth)
    block_second = (epi_block.astype(jnp.float32) + jax.nn.silu(block_out)).astype(jnp.bfloat16)
    views_all = block_second.shape[2]
    second_views = lax.all_to_all(block_second, "ang", split_axis=2, concat_axis=3, tiled=True)
    lifted_views = project_up(upsample_weight, second_views)
    up_grad = jnp.einsum(
        "buvhsw,buvhcw->sc", cotangent, second_views, preferred_element_type=jnp.float32
    )
    view_grad = jnp.einsum(
        "sc,buvhsw->buvhcw", upsample_weight, cotangent, preferred_element_type=jnp.float32
    ).astype(jnp.bfloat16)
    second_grad = lax.all_to_all(view_grad, "ang", split_axis=3, concat_axis=2, tiled=True)
    epi_slope = (second_grad.astype(jnp.float32) * silu_slope(block_out)).astype(jnp.bfloat16)
    epi_grad = weight_grad(epi_slope, padded_block, 2, views_all, breadth)
    slope_pad = jnp.pad(epi_slope, ((0, 0), (0, 0), (1, 1), (0, 0), (0, 0), (1, 1)))
    first_grad = (
        second_grad.astype(jnp.float32) + epi_back(slope_pad, epi_weight, views_all, breadth)
    ).astype(jnp.bfloat16)
    first_views = lax.all_to_all(first_grad, "ang", split_axis=2, concat_axis=3, tiled=True)
    upscaled = lifted_views.reshape(
        batch_here, angular_rows, views_here, rows_here, SCALE, SCALE, breadth
    )
    upscaled = upscaled.transpose(0, 1, 2, 3, 4, 6, 5).reshape(
        batch_here, angular_rows, views_here, rows_here * SCALE, breadth * SCALE
    )
    spatial_slope = (first_views.astype(jnp.float32) * silu_slope(spatial_out)).astype(jnp.bfloat16)
    spatial_grad = weight_grad(spatial_slope, spatial_in, 3, rows_here, breadth)
    spatial_grad, epi_grad, up_grad = sum_everywhere((spatial_grad, epi_grad, up_grad))
    return (upscaled, spatial_grad, epi_grad, up_grad)


def solution(mesh):
    placed = (
        P("dp", None, "ang", "rows", None, None),
        P(),
        P(),
        P(),
        P("dp", None, "ang", "rows", None),
    )
    return jax.shard_map(
        on_device,
        mesh=mesh,
        in_specs=placed,
        out_specs=(P("dp", None, "ang", "rows", None), P(), P(), P()),
        check_vma=False,
    )
```

profile of v0, /device:TPU:1, one launch (start us, length us, event | category | flops | bytes accessed | tf_op | source)
XLA Modules:
  0.0 144.1 jit_solution(14145591861268365492)
XLA Ops:
  1.6 4.0 %collective-permute-start = (bf16[1,1,2,1,64,512]{5,4,3,2,1,0:T(8,128)(2,1)S(1)}, bf16[1,1,2,1,64,512]{5,4,3,2,1,0:T(8,128)(2,1)S(1)}, u32[]{:S(2)}, u32[]{:S(2)}) collective-permute-start(bf16[1,1,2,1,64,512]{5,4,3,2,1,0:T(8,128)(2,1)S(1)} %get-tuple-element.14), channel_id=1, source_target_pairs={{0,1},{1,2},{2,3},{3,4},{4,5},{5,6},{6,7},{7,8},{8,9},{9,10},{10,1... | collective-permute-start | bytes 393224 | tf_op jit(solution)/shard_map/ppermute | solution.py:18
  5.6 1.3 collective-permute-start.1
  6.9 10.8 %reshape.280 = bf16[1,1,2,4,4,512,4]{6,5,4,3,2,1,0:T(8,128)(2,1)} reshape(bf16[1,1,2,16,2048]{4,3,2,1,0:T(8,128)(2,1)} %param.9) | data formatting | bytes 262144 | tf_op jit(solution)/shard_map/reshape | solution.py:171
  17.7 3.7 %copy.156 = bf16[1,1,2,4,4,4,512]{6,3,5,4,2,1,0:T(4,128)(2,1)S(1)} copy(bf16[1,1,2,4,4,4,512]{5,6,4,3,2,1,0:T(8,128)(2,1)} %bitcast.472) | data formatting | bytes 262144 | tf_op jit(solution)/shard_map/transpose | solution.py:174
  22.6 4.2 %all-to-all-start.2 = ((bf16[1,1,2,4,64,512]{5,4,2,1,0,3:T(8,128)(2,1)}), bf16[1,1,2,4,64,512]{5,4,2,1,0,3:T(8,128)(2,1)S(1)}, u32[]{:S(2)}, u32[]{:S(2)}) async-start(bf16[1,1,2,4,64,512]{5,4,2,1,0,3:T(8,128)(2,1)} %copy.158), calls=%async_computation.2 | async-start | bytes 1048576 | tf_op jit(solution)/shard_map/all_to_all | solution.py:191
  30.1 1.5 %add_convert_fusion.1 = (bf16[1,1,2,4,64,512]{5,4,3,2,1,0:T(8,128)(2,1)S(1)}, f32[1,1,2,4,64,512]{5,4,3,2,1,0:T(8,128)}) fusion(bf16[1,1,2,4,64,512]{5,4,3,2,1,0:T(8,128)(2,1)S(1)} %copy-done.1, f32[2,4,512,64]{2,3,1,0:T(8,128)S(1)} %fusion.113, f32[2,4,512,64]{2,3,1,0:T(8,128)S(1)} %convolution_add_fusion.9, ...), kind=kOutput, calls=%fused_computation.80 | convolution fusion | flops 35913728 | bytes 4734976 | tf_op jit(solution)/shard_map/oc,buvhcw->buvhow/dot_general | solution.py:36
  32.4 2.3 %all-to-all-done.2 = bf16[1,1,2,4,64,512]{5,4,2,1,0,3:T(8,128)(2,1)S(1)} async-done(((bf16[1,1,2,4,64,512]{5,4,2,1,0,3:T(8,128)(2,1)}), bf16[1,1,2,4,64,512]{5,4,2,1,0,3:T(8,128)(2,1)S(1)}, u32[]{:S(2)}, u32[]{:S(2)}) %all-to-all-start.2) | async-done | bytes 524320 | tf_op jit(solution)/shard_map/all_to_all | solution.py:191
  35.6 3.6 %all-to-all-start = ((bf16[1,1,2,4,64,512]{5,4,2,1,0,3:T(8,128)(2,1)}), bf16[1,1,2,4,64,512]{5,4,2,1,0,3:T(8,128)(2,1)S(1)}, u32[]{:S(2)}, u32[]{:S(2)}) async-start(bf16[1,1,2,4,64,512]{5,4,2,1,0,3:T(8,128)(2,1)} %copy.152), calls=%async_computation | async-start | bytes 1048576 | tf_op jit(solution)/shard_map/all_to_all | solution.py:177
  39.2 2.3 %slice_bitcast_fusion.5 = (bf16[2,4,64,512]{3,2,1,0:T(8,128)(2,1)}, bf16[2,4,64,512]{3,2,1,0:T(8,128)(2,1)}, bf16[2,4,64,512]{3,2,1,0:T(8,128)(2,1)}, bf16[2,4,6...) fusion(bf16[1,1,2,6,64,514]{5,4,3,2,1,0:T(8,128)(2,1)S(1)} %fusion.15), kind=kLoop, calls=%fused_computation.110 | loop fusion | bytes 6291456 | tf_op jit(solution)/shard_map/reshape
  41.7 4.3 %all-to-all-done = bf16[1,1,2,4,64,512]{5,4,2,1,0,3:T(8,128)(2,1)S(1)} async-done(((bf16[1,1,2,4,64,512]{5,4,2,1,0,3:T(8,128)(2,1)}), bf16[1,1,2,4,64,512]{5,4,2,1,0,3:T(8,128)(2,1)S(1)}, u32[]{:S(2)}, u32[]{:S(2)}) %all-to-all-start) | async-done | bytes 524320 | tf_op jit(solution)/shard_map/all_to_all | solution.py:177
  48.6 1.6 %multiply_convert_fusion = (bf16[1,1,8,1,64,512]{5,4,2,3,1,0:T(8,128)(2,1)S(1)}, bf16[1,1,8,1,64,512]{5,4,3,1,0,2:T(8,128)(2,1)}) fusion(f32[1,1,8,1,64,512]{5,4,2,3,1,0:T(8,128)S(1)} %bitcast.475, bf16[1,1,8,1,64,512]{5,4,2,3,1,0:T(8,128)(2,1)S(1)} %bitcast.461, f32[8,512,64]{1,2,0:T(8,128)S(1)} %convolution_add_fusion.1, ...), kind=kOutput, calls=%fused_computation.77 | convolution fusion | flops 37224448 | bytes 4210688 | tf_op jit(solution)/shard_map/oc,buvhcw->buvhow/dot_general | solution.py:51
  57.4 3.5 %all-to-all-start.3 = ((bf16[1,1,8,1,64,512]{5,4,3,1,0,2:T(8,128)(2,1)}), bf16[1,1,8,1,64,512]{5,4,3,1,0,2:T(8,128)(2,1)S(1)}, u32[]{:S(2)}, u32[]{:S(2)}) async-start(bf16[1,1,8,1,64,512]{5,4,3,1,0,2:T(8,128)(2,1)} %fusion.8), calls=%async_computation.3 | async-start | bytes 1048576 | tf_op jit(solution)/shard_map/all_to_all | solution.py:198
  61.5 6.3 %all-to-all-done.3 = bf16[1,1,8,1,64,512]{5,4,3,1,0,2:T(8,128)(2,1)S(1)} async-done(((bf16[1,1,8,1,64,512]{5,4,3,1,0,2:T(8,128)(2,1)}), bf16[1,1,8,1,64,512]{5,4,3,1,0,2:T(8,128)(2,1)S(1)}, u32[]{:S(2)}, u32[]{:S(2)}) %all-to-all-start.3) | async-done | bytes 524320 | tf_op jit(solution)/shard_map/all_to_all | solution.py:198
  67.8 3.5 %all-to-all-start.1 = ((bf16[1,1,8,1,64,512]{5,4,3,1,0,2:T(8,128)(2,1)}), bf16[1,1,8,1,64,512]{5,4,3,1,0,2:T(8,128)(2,1)S(1)}, u32[]{:S(2)}, u32[]{:S(2)}) async-start(bf16[1,1,8,1,64,512]{5,4,3,1,0,2:T(8,128)(2,1)} %get-tuple-element.5), calls=%async_computation.1 | async-start | bytes 1048576 | tf_op jit(solution)/shard_map/all_to_all | solution.py:183
  75.0 3.1 %all-to-all-done.1 = bf16[1,1,8,1,64,512]{5,4,3,1,0,2:T(8,128)(2,1)S(1)} async-done(((bf16[1,1,8,1,64,512]{5,4,3,1,0,2:T(8,128)(2,1)}), bf16[1,1,8,1,64,512]{5,4,3,1,0,2:T(8,128)(2,1)S(1)}, u32[]{:S(2)}, u32[]{:S(2)}) %all-to-all-start.1) | async-done | bytes 524320 | tf_op jit(solution)/shard_map/all_to_all | solution.py:183
  78.6 1.7 %collective-permute-start.2 = (f32[152,128]{1,0:T(8,128)S(1)}, f32[152,128]{1,0:T(8,128)S(1)}, u32[]{:S(2)}, u32[]{:S(2)}) collective-permute-start(f32[152,128]{1,0:T(8,128)S(1)} %get-tuple-element.24), channel_id=1, source_target_pairs={{0,128},{64,192},{128,0},{192,64},{1,129},{65,193},{129,1},{193,65... | collective-permute-start | bytes 233480 | tf_op jit(solution)/shard_map/ppermute | solution.py:122
  80.3 6.1 %collective-permute-start.3 = (f32[152,128]{1,0:T(8,128)S(1)}, f32[152,128]{1,0:T(8,128)S(1)}, u32[]{:S(2)}, u32[]{:S(2)}) collective-permute-start(f32[152,128]{1,0:T(8,128)S(1)} %get-tuple-element.23), channel_id=1, source_target_pairs={{0,64},{64,128},{128,192},{192,0},{1,65},{65,129},{129,193},{193,1... | collective-permute-start | bytes 233480 | tf_op jit(solution)/shard_map/ppermute | solution.py:122
  86.5 1.8 %collective-permute-done.3 = f32[152,128]{1,0:T(8,128)S(1)} collective-permute-done((f32[152,128]{1,0:T(8,128)S(1)}, f32[152,128]{1,0:T(8,128)S(1)}, u32[]{:S(2)}, u32[]{:S(2)}) %collective-permute-start.3) | collective-permute-done | bytes 77856 | tf_op jit(solution)/shard_map/ppermute | solution.py:122
  88.3 2.1 %collective-permute-done.4 = f32[152,128]{1,0:T(8,128)S(1)} collective-permute-done((f32[152,128]{1,0:T(8,128)S(1)}, f32[152,128]{1,0:T(8,128)S(1)}, u32[]{:S(2)}, u32[]{:S(2)}) %collective-permute-start.4) | collective-permute-done | bytes 77856 | tf_op jit(solution)/shard_map/ppermute | solution.py:122
  90.5 3.7 %collective-permute-start.5 = (f32[152,128]{1,0:T(8,128)S(1)}, f32[152,128]{1,0:T(8,128)S(1)}, u32[]{:S(2)}, u32[]{:S(2)}) collective-permute-start(f32[152,128]{1,0:T(8,128)S(1)} %fusion.85), channel_id=1, source_target_pairs={{0,2},{1,3},{2,0},{3,1},{4,6},{5,7},{6,4},{7,5},{8,10},{9,11},{10,... | collective-permute-start | bytes 233480 | tf_op jit(solution)/shard_map/ppermute | solution.py:122
  94.1 1.8 %collective-permute-start.6 = (f32[152,128]{1,0:T(8,128)S(1)}, f32[152,128]{1,0:T(8,128)S(1)}, u32[]{:S(2)}, u32[]{:S(2)}) collective-permute-start(f32[152,128]{1,0:T(8,128)S(1)} %fusion.85), channel_id=1, source_target_pairs={{0,1},{1,2},{2,3},{3,0},{4,5},{5,6},{6,7},{7,4},{8,9},{9,10},{10,1... | collective-permute-start | bytes 233480 | tf_op jit(solution)/shard_map/ppermute | solution.py:122
  96.8 1.8 %collective-permute-done.6 = f32[152,128]{1,0:T(8,128)S(1)} collective-permute-done((f32[152,128]{1,0:T(8,128)S(1)}, f32[152,128]{1,0:T(8,128)S(1)}, u32[]{:S(2)}, u32[]{:S(2)}) %collective-permute-start.6) | collective-permute-done | bytes 77856 | tf_op jit(solution)/shard_map/ppermute | solution.py:122
  99.7 7.5 %collective-permute-start.10 = (f32[152,128]{1,0:T(8,128)S(1)}, f32[152,128]{1,0:T(8,128)S(1)}, u32[]{:S(2)}, u32[]{:S(2)}) collective-permute-start(f32[152,128]{1,0:T(8,128)S(1)} %add_add_fusion.2), channel_id=1, source_target_pairs={{0,12},{4,0},{8,4},{12,8},{1,13},{5,1},{9,5},{13,9},{2,14},{6,2},{... | collective-permute-start | bytes 233480 | tf_op jit(solution)/shard_map/ppermute | solution.py:122
  107.2 2.2 %collective-permute-start.8 = (f32[152,128]{1,0:T(8,128)S(1)}, f32[152,128]{1,0:T(8,128)S(1)}, u32[]{:S(2)}, u32[]{:S(2)}) collective-permute-start(f32[152,128]{1,0:T(8,128)S(1)} %add_add_fusion.2), channel_id=1, source_target_pairs={{0,8},{4,12},{8,0},{12,4},{1,9},{5,13},{9,1},{13,5},{2,10},{6,14},... | collective-permute-start | bytes 233480 | tf_op jit(solution)/shard_map/ppermute | solution.py:122
  109.4 2.3 %collective-permute-start.9 = (f32[152,128]{1,0:T(8,128)S(1)}, f32[152,128]{1,0:T(8,128)S(1)}, u32[]{:S(2)}, u32[]{:S(2)}) collective-permute-start(f32[152,128]{1,0:T(8,128)S(1)} %add_add_fusion.2), channel_id=1, source_target_pairs={{0,4},{4,8},{8,12},{12,0},{1,5},{5,9},{9,13},{13,1},{2,6},{6,10},{... | collective-permute-start | bytes 233480 | tf_op jit(solution)/shard_map/ppermute | solution.py:122
  111.7 2.8 %collective-permute-done.8 = f32[152,128]{1,0:T(8,128)S(1)} collective-permute-done((f32[152,128]{1,0:T(8,128)S(1)}, f32[152,128]{1,0:T(8,128)S(1)}, u32[]{:S(2)}, u32[]{:S(2)}) %collective-permute-start.8) | collective-permute-done | bytes 77856 | tf_op jit(solution)/shard_map/ppermute | solution.py:122
  114.5 1.5 %collective-permute-done.9 = f32[152,128]{1,0:T(8,128)S(1)} collective-permute-done((f32[152,128]{1,0:T(8,128)S(1)}, f32[152,128]{1,0:T(8,128)S(1)}, u32[]{:S(2)}, u32[]{:S(2)}) %collective-permute-start.9) | collective-permute-done | bytes 77856 | tf_op jit(solution)/shard_map/ppermute | solution.py:122
  117.6 1.5 %collective-permute-start.13 = (f32[152,128]{1,0:T(8,128)S(1)}, f32[152,128]{1,0:T(8,128)S(1)}, u32[]{:S(2)}, u32[]{:S(2)}) collective-permute-start(f32[152,128]{1,0:T(8,128)S(1)} %add_add_fusion.1), channel_id=1, source_target_pairs={{0,48},{16,0},{32,16},{48,32},{1,49},{17,1},{33,17},{49,33},{2,50}... | collective-permute-start | bytes 233480 | tf_op jit(solution)/shard_map/ppermute | solution.py:122
  119.1 1.9 %collective-permute-done.11 = f32[152,128]{1,0:T(8,128)S(1)} collective-permute-done((f32[152,128]{1,0:T(8,128)S(1)}, f32[152,128]{1,0:T(8,128)S(1)}, u32[]{:S(2)}, u32[]{:S(2)}) %collective-permute-start.11) | collective-permute-done | bytes 77856 | tf_op jit(solution)/shard_map/ppermute | solution.py:122
  121.7 6.1 %collective-permute-start.14 = (f32[152,128]{1,0:T(8,128)S(1)}, f32[152,128]{1,0:T(8,128)S(1)}, u32[]{:S(2)}, u32[]{:S(2)}) collective-permute-start(f32[152,128]{1,0:T(8,128)S(1)} %add_add_fusion), channel_id=1, source_target_pairs={{0,64},{64,128},{128,192},{192,0},{1,65},{65,129},{129,193},{193,1... | collective-permute-start | bytes 233480 | tf_op jit(solution)/shard_map/ppermute | solution.py:122
  128.6 3.3 %copy.155 = bf16[1,1,2,4,4,4,512]{5,6,4,3,2,1,0:T(8,128)(2,1)} copy(bf16[1,1,2,4,4,4,512]{6,5,4,3,2,1,0:T(4,128)(2,1)S(1)} %reshape.278) | data formatting | bytes 262144 | tf_op jit(solution)/shard_map/reshape | solution.py:199
  131.9 9.7 %reshape.279 = bf16[1,1,2,16,2048]{4,3,2,1,0:T(8,128)(2,1)} reshape(bf16[1,1,2,4,4,512,4]{6,5,4,3,2,1,0:T(8,128)(2,1)} %bitcast.471) | data formatting | bytes 262144 | tf_op jit(solution)/shard_map/reshape | solution.py:202
  (128 shorter events, 28.9 us)
Async XLA Ops:
  0.6 20.8 %copy-start = (bf16[16,64]{1,0:T(8,128)(2,1)S(1)}, bf16[16,64]{1,0:T(8,128)(2,1)}, u32[]{:S(2)}) copy-start(bf16[16,64]{1,0:T(8,128)(2,1)} %param.8) | copy-start | bytes 6148
  1.6 25.1 %collective-permute-start = (bf16[1,1,2,1,64,512]{5,4,3,2,1,0:T(8,128)(2,1)S(1)}, bf16[1,1,2,1,64,512]{5,4,3,2,1,0:T(8,128)(2,1)S(1)}, u32[]{:S(2)}, u32[]{:S(2)}) collective-permute-start(bf16[1,1,2,1,64,512]{5,4,3,2,1,0:T(8,128)(2,1)S(1)} %get-tuple-element.14), channel_id=1, source_target_pairs={{0,1},{1,2},{2,3},{3,4},{4,5},{5,6},{6,7},{7,8},{8,9},{9,10},{10,1... | collective-permute-start | bytes 393224 | tf_op jit(solution)/shard_map/ppermute | solution.py:18
  5.6 21.2 %collective-permute-start.1 = (bf16[1,1,2,1,64,512]{5,4,3,2,1,0:T(8,128)(2,1)S(1)}, bf16[1,1,2,1,64,512]{5,4,3,2,1,0:T(8,128)(2,1)S(1)}, u32[]{:S(2)}, u32[]{:S(2)}) collective-permute-start(bf16[1,1,2,1,64,512]{5,4,3,2,1,0:T(8,128)(2,1)S(1)} %get-tuple-element.15), channel_id=1, source_target_pairs={{1,0},{2,1},{3,2},{4,3},{5,4},{6,5},{7,6},{8,7},{9,8},{10,9},{11,1... | collective-permute-start | bytes 393224 | tf_op jit(solution)/shard_map/ppermute | solution.py:20
  21.4 5.4 %copy-start.1 = (bf16[1,1,2,4,64,512]{5,4,3,2,1,0:T(8,128)(2,1)S(1)}, bf16[1,1,2,4,64,512]{5,4,3,2,1,0:T(8,128)(2,1)}, u32[]{:S(2)}) copy-start(bf16[1,1,2,4,64,512]{5,4,3,2,1,0:T(8,128)(2,1)} %param.5) | copy-start | bytes 1572868
  21.8 5.6 %copy-start.16 = (bf16[3,3,64,64]{3,2,1,0:T(8,128)(2,1)S(1)}, bf16[3,3,64,64]{3,2,1,0:T(8,128)(2,1)}, u32[]{:S(2)}) copy-start(bf16[3,3,64,64]{3,2,1,0:T(8,128)(2,1)} %param.6) | copy-start | bytes 221188
  22.6 12.2 %all-to-all-start.2 = ((bf16[1,1,2,4,64,512]{5,4,2,1,0,3:T(8,128)(2,1)}), bf16[1,1,2,4,64,512]{5,4,2,1,0,3:T(8,128)(2,1)S(1)}, u32[]{:S(2)}, u32[]{:S(2)}) async-start(bf16[1,1,2,4,64,512]{5,4,2,1,0,3:T(8,128)(2,1)} %copy.158), calls=%async_computation.2 | async-start | bytes 1048576 | tf_op jit(solution)/shard_map/all_to_all | solution.py:191
  27.7 2.4 %copy-start.8 = (bf16[2,4,64,512]{3,2,1,0:T(8,128)(2,1)}, bf16[2,4,64,512]{3,2,1,0:T(8,128)(2,1)S(1)}, u32[]{:S(2)}) copy-start(bf16[2,4,64,512]{3,2,1,0:T(8,128)(2,1)S(1)} %get-tuple-element.12) | copy-start | bytes 1572868
  35.6 10.4 %all-to-all-start = ((bf16[1,1,2,4,64,512]{5,4,2,1,0,3:T(8,128)(2,1)}), bf16[1,1,2,4,64,512]{5,4,2,1,0,3:T(8,128)(2,1)S(1)}, u32[]{:S(2)}, u32[]{:S(2)}) async-start(bf16[1,1,2,4,64,512]{5,4,2,1,0,3:T(8,128)(2,1)} %copy.152), calls=%async_computation | async-start | bytes 1048576 | tf_op jit(solution)/shard_map/all_to_all | solution.py:177
  39.2 2.3 %copy-start.5 = (bf16[1,1,2,4,64,512]{5,4,2,1,0,3:T(8,128)(2,1)S(1)}, bf16[1,1,2,4,64,512]{5,4,2,1,0,3:T(8,128)(2,1)}, u32[]{:S(2)}) copy-start(bf16[1,1,2,4,64,512]{5,4,2,1,0,3:T(8,128)(2,1)} %copy-done.4) | copy-start | bytes 1572868
  39.2 6.7 %copy-start.7 = (bf16[3,3,64,64]{3,2,1,0:T(8,128)(2,1)S(1)}, bf16[3,3,64,64]{3,2,1,0:T(8,128)(2,1)}, u32[]{:S(2)}) copy-start(bf16[3,3,64,64]{3,2,1,0:T(8,128)(2,1)} %param.7) | copy-start | bytes 221188
  57.4 10.4 %all-to-all-start.3 = ((bf16[1,1,8,1,64,512]{5,4,3,1,0,2:T(8,128)(2,1)}), bf16[1,1,8,1,64,512]{5,4,3,1,0,2:T(8,128)(2,1)S(1)}, u32[]{:S(2)}, u32[]{:S(2)}) async-start(bf16[1,1,8,1,64,512]{5,4,3,1,0,2:T(8,128)(2,1)} %fusion.8), calls=%async_computation.3 | async-start | bytes 1048576 | tf_op jit(solution)/shard_map/all_to_all | solution.py:198
  61.3 10.0 %copy-start.6 = (f32[1,1,2,4,64,512]{5,4,3,2,1,0:T(8,128)S(1)}, f32[1,1,2,4,64,512]{5,4,3,2,1,0:T(8,128)}, u32[]{:S(2)}) copy-start(f32[1,1,2,4,64,512]{5,4,3,2,1,0:T(8,128)} %get-tuple-element.26) | copy-start | bytes 3145732
  61.3 10.4 %copy-start.3 = (bf16[2,4,64,512]{3,2,1,0:T(8,128)(2,1)S(1)}, bf16[2,4,64,512]{3,2,1,0:T(8,128)(2,1)}, u32[]{:S(2)}) copy-start(bf16[2,4,64,512]{3,2,1,0:T(8,128)(2,1)} %copy-done.2) | copy-start | bytes 1572868
  67.8 10.4 %all-to-all-start.1 = ((bf16[1,1,8,1,64,512]{5,4,3,1,0,2:T(8,128)(2,1)}), bf16[1,1,8,1,64,512]{5,4,3,1,0,2:T(8,128)(2,1)S(1)}, u32[]{:S(2)}, u32[]{:S(2)}) async-start(bf16[1,1,8,1,64,512]{5,4,3,1,0,2:T(8,128)(2,1)} %get-tuple-element.5), calls=%async_computation.1 | async-start | bytes 1048576 | tf_op jit(solution)/shard_map/all_to_all | solution.py:183
  72.0 1.1 copy-start.14
  72.3 1.1 copy-start.13
  72.8 1.1 copy-start.12
  78.6 7.9 %collective-permute-start.2 = (f32[152,128]{1,0:T(8,128)S(1)}, f32[152,128]{1,0:T(8,128)S(1)}, u32[]{:S(2)}, u32[]{:S(2)}) collective-permute-start(f32[152,128]{1,0:T(8,128)S(1)} %get-tuple-element.24), channel_id=1, source_target_pairs={{0,128},{64,192},{128,0},{192,64},{1,129},{65,193},{129,1},{193,65... | collective-permute-start | bytes 233480 | tf_op jit(solution)/shard_map/ppermute | solution.py:122
  80.3 8.0 %collective-permute-start.3 = (f32[152,128]{1,0:T(8,128)S(1)}, f32[152,128]{1,0:T(8,128)S(1)}, u32[]{:S(2)}, u32[]{:S(2)}) collective-permute-start(f32[152,128]{1,0:T(8,128)S(1)} %get-tuple-element.23), channel_id=1, source_target_pairs={{0,64},{64,128},{128,192},{192,0},{1,65},{65,129},{129,193},{193,1... | collective-permute-start | bytes 233480 | tf_op jit(solution)/shard_map/ppermute | solution.py:122
  86.4 4.1 %collective-permute-start.4 = (f32[152,128]{1,0:T(8,128)S(1)}, f32[152,128]{1,0:T(8,128)S(1)}, u32[]{:S(2)}, u32[]{:S(2)}) collective-permute-start(f32[152,128]{1,0:T(8,128)S(1)} %get-tuple-element.22), channel_id=1, source_target_pairs={{0,192},{64,0},{128,64},{192,128},{1,193},{65,1},{129,65},{193,129... | collective-permute-start | bytes 233480 | tf_op jit(solution)/shard_map/ppermute | solution.py:122
  90.5 6.4 %collective-permute-start.5 = (f32[152,128]{1,0:T(8,128)S(1)}, f32[152,128]{1,0:T(8,128)S(1)}, u32[]{:S(2)}, u32[]{:S(2)}) collective-permute-start(f32[152,128]{1,0:T(8,128)S(1)} %fusion.85), channel_id=1, source_target_pairs={{0,2},{1,3},{2,0},{3,1},{4,6},{5,7},{6,4},{7,5},{8,10},{9,11},{10,... | collective-permute-start | bytes 233480 | tf_op jit(solution)/shard_map/ppermute | solution.py:122
  94.1 4.5 %collective-permute-start.6 = (f32[152,128]{1,0:T(8,128)S(1)}, f32[152,128]{1,0:T(8,128)S(1)}, u32[]{:S(2)}, u32[]{:S(2)}) collective-permute-start(f32[152,128]{1,0:T(8,128)S(1)} %fusion.85), channel_id=1, source_target_pairs={{0,1},{1,2},{2,3},{3,0},{4,5},{5,6},{6,7},{7,4},{8,9},{9,10},{10,1... | collective-permute-start | bytes 233480 | tf_op jit(solution)/shard_map/ppermute | solution.py:122
  95.9 3.7 %collective-permute-start.7 = (f32[152,128]{1,0:T(8,128)S(1)}, f32[152,128]{1,0:T(8,128)S(1)}, u32[]{:S(2)}, u32[]{:S(2)}) collective-permute-start(f32[152,128]{1,0:T(8,128)S(1)} %fusion.85), channel_id=1, source_target_pairs={{0,3},{1,0},{2,1},{3,2},{4,7},{5,4},{6,5},{7,6},{8,11},{9,8},{10,9... | collective-permute-start | bytes 233480 | tf_op jit(solution)/shard_map/ppermute | solution.py:122
  99.7 12.0 %collective-permute-start.10 = (f32[152,128]{1,0:T(8,128)S(1)}, f32[152,128]{1,0:T(8,128)S(1)}, u32[]{:S(2)}, u32[]{:S(2)}) collective-permute-start(f32[152,128]{1,0:T(8,128)S(1)} %add_add_fusion.2), channel_id=1, source_target_pairs={{0,12},{4,0},{8,4},{12,8},{1,13},{5,1},{9,5},{13,9},{2,14},{6,2},{... | collective-permute-start | bytes 233480 | tf_op jit(solution)/shard_map/ppermute | solution.py:122
  107.2 7.3 %collective-permute-start.8 = (f32[152,128]{1,0:T(8,128)S(1)}, f32[152,128]{1,0:T(8,128)S(1)}, u32[]{:S(2)}, u32[]{:S(2)}) collective-permute-start(f32[152,128]{1,0:T(8,128)S(1)} %add_add_fusion.2), channel_id=1, source_target_pairs={{0,8},{4,12},{8,0},{12,4},{1,9},{5,13},{9,1},{13,5},{2,10},{6,14},... | collective-permute-start | bytes 233480 | tf_op jit(solution)/shard_map/ppermute | solution.py:122
  109.4 6.6 %collective-permute-start.9 = (f32[152,128]{1,0:T(8,128)S(1)}, f32[152,128]{1,0:T(8,128)S(1)}, u32[]{:S(2)}, u32[]{:S(2)}) collective-permute-start(f32[152,128]{1,0:T(8,128)S(1)} %add_add_fusion.2), channel_id=1, source_target_pairs={{0,4},{4,8},{8,12},{12,0},{1,5},{5,9},{9,13},{13,1},{2,6},{6,10},{... | collective-permute-start | bytes 233480 | tf_op jit(solution)/shard_map/ppermute | solution.py:122
  116.0 4.9 %collective-permute-start.11 = (f32[152,128]{1,0:T(8,128)S(1)}, f32[152,128]{1,0:T(8,128)S(1)}, u32[]{:S(2)}, u32[]{:S(2)}) collective-permute-start(f32[152,128]{1,0:T(8,128)S(1)} %add_add_fusion.1), channel_id=1, source_target_pairs={{0,32},{16,48},{32,0},{48,16},{1,33},{17,49},{33,1},{49,17},{2,34}... | collective-permute-start | bytes 233480 | tf_op jit(solution)/shard_map/ppermute | solution.py:122
  116.4 5.3 %collective-permute-start.12 = (f32[152,128]{1,0:T(8,128)S(1)}, f32[152,128]{1,0:T(8,128)S(1)}, u32[]{:S(2)}, u32[]{:S(2)}) collective-permute-start(f32[152,128]{1,0:T(8,128)S(1)} %add_add_fusion.1), channel_id=1, source_target_pairs={{0,16},{16,32},{32,48},{48,0},{1,17},{17,33},{33,49},{49,1},{2,18}... | collective-permute-start | bytes 233480 | tf_op jit(solution)/shard_map/ppermute | solution.py:122
  117.6 4.1 %collective-permute-start.13 = (f32[152,128]{1,0:T(8,128)S(1)}, f32[152,128]{1,0:T(8,128)S(1)}, u32[]{:S(2)}, u32[]{:S(2)}) collective-permute-start(f32[152,128]{1,0:T(8,128)S(1)} %add_add_fusion.1), channel_id=1, source_target_pairs={{0,48},{16,0},{32,16},{48,32},{1,49},{17,1},{33,17},{49,33},{2,50}... | collective-permute-start | bytes 233480 | tf_op jit(solution)/shard_map/ppermute | solution.py:122
  121.7 19.9 %collective-permute-start.14 = (f32[152,128]{1,0:T(8,128)S(1)}, f32[152,128]{1,0:T(8,128)S(1)}, u32[]{:S(2)}, u32[]{:S(2)}) collective-permute-start(f32[152,128]{1,0:T(8,128)S(1)} %add_add_fusion), channel_id=1, source_target_pairs={{0,64},{64,128},{128,192},{192,0},{1,65},{65,129},{129,193},{193,1... | collective-permute-start | bytes 233480 | tf_op jit(solution)/shard_map/ppermute | solution.py:122
  127.9 13.7 %collective-permute-start.15 = (f32[152,128]{1,0:T(8,128)S(1)}, f32[152,128]{1,0:T(8,128)S(1)}, u32[]{:S(2)}, u32[]{:S(2)}) collective-permute-start(f32[152,128]{1,0:T(8,128)S(1)} %add_add_fusion), channel_id=1, source_target_pairs={{0,128},{64,192},{128,0},{192,64},{1,129},{65,193},{129,1},{193,65... | collective-permute-start | bytes 233480 | tf_op jit(solution)/shard_map/ppermute | solution.py:122
  127.9 13.7 %collective-permute-start.16 = (f32[152,128]{1,0:T(8,128)S(1)}, f32[152,128]{1,0:T(8,128)S(1)}, u32[]{:S(2)}, u32[]{:S(2)}) collective-permute-start(f32[152,128]{1,0:T(8,128)S(1)} %add_add_fusion), channel_id=1, source_target_pairs={{0,192},{64,0},{128,64},{192,128},{1,193},{65,1},{129,65},{193,129... | collective-permute-start | bytes 233480 | tf_op jit(solution)/shard_map/ppermute | solution.py:122
  (6 other events, 6.0 us)
where the time goes:
time: 145 us; the launch traced here: 144 us
  starting transfers between devices  56 us (39%)
  local copies, waits for them, and re-layouts  36.7 us (25%)
  waiting for transfers between devices  29.8 us (21%)
  matrix products  18.9 us (13%)
    ppermute x15, starting transfers between devices, shifted(): return lax.ppermute(value, axis, pairs)  35.9 us
    ppermute x15, waiting for transfers between devices, shifted(): return lax.ppermute(value, axis, pairs)  13.7 us
    reshape x1, local copies, waits for them, and re-layouts, on_device(): image_grad.reshape(batch_here, angular_rows, views_here, rows_here, SCALE...  10.8 us
    reshape x1, local copies, waits for them, and re-layouts, on_device(): upscaled.transpose(0, 1, 2, 3, 4, 6, 5)  9.74 us
    all_to_all x1, waiting for transfers between devices, on_device(): lax.all_to_all(first_grad, 'ang', split_axis=2, concat_axis=3, tiled=True)  6.33 us
    dot_general x18, matrix products, weight_grad(): jnp.einsum('buvhow,buvhcw->oc', upstream, window, preferred_element_type=...  5.51 us
    dot_general x9, matrix products, epi_back(): jnp.einsum('oc,buvhow->buvhcw', weight[tap_row, tap_col], padded[:, :, 2...  4.45 us
    all_to_all x1, waiting for transfers between devices, on_device(): lax.all_to_all(first, 'ang', split_axis=3, concat_axis=2, tiled=True)  4.28 us
  transfers between devices with their start and end apart: 21, of which 12 were waited for; matrix products, arithmetic and copies ran while one was open for 28% of the time, Pallas kernels for 0%

commit v1 on v0

--- a/solution.py
+++ b/solution.py
@@ -188,7 +188,10 @@
     view_grad = jnp.einsum(
         "sc,buvhsw->buvhcw", upsample_weight, cotangent, preferred_element_type=jnp.float32
     ).astype(jnp.bfloat16)
-    second_grad = lax.all_to_all(view_grad, "ang", split_axis=3, concat_axis=2, tiled=True)
+    size = lax.axis_size("ang")
+    blocks = jnp.stack(jnp.split(view_grad, size, axis=3), axis=0)
+    blocks = lax.all_to_all(blocks, "ang", split_axis=0, concat_axis=0)
+    second_grad = jnp.concatenate(blocks, axis=2)
     epi_slope = (second_grad.astype(jnp.float32) * silu_slope(block_out)).astype(jnp.bfloat16)
     epi_grad = weight_grad(epi_slope, padded_block, 2, views_all, breadth)
     slope_pad = jnp.pad(epi_slope, ((0, 0), (0, 0), (1, 1), (0, 0), (0, 0), (1, 1)))

time: 145 us -> 149 us (1.028)
  matrix products: 18.9 us -> 22.7 us
  local copies, waits for them, and re-layouts: 36.7 us -> 35 us
    dot_general x9, matrix products: 4.24 us -> 6.5 us  [epi_conv(): jnp.einsum('oc,buvhcw->buvhow', weight[tap_row, tap_col], padded[:, :, ta...]
    dot_general x9, matrix products: 3.95 us -> 5.47 us  [spatial_conv(): jnp.einsum('oc,buvhcw->buvhow', weight[tap_row, tap_col], padded[:, :, :,...]
  transfers between devices with their start and end apart: 21 -> 21, of which waited for: 12 -> 12; matrix products, arithmetic and copies ran while one was open for 28% -> 26% of each run, Pallas kernels for 0% -> 0%
where the time goes in v1:
time: 149 us; the launch traced here: 148 us
  starting transfers between devices  56 us (38%)
  local copies, waits for them, and re-layouts  35 us (23%)
  waiting for transfers between devices  31.1 us (21%)
  matrix products  22.7 us (15%)
  other arithmetic  2.17 us (1%)
    ppermute x15, starting transfers between devices, shifted(): return lax.ppermute(value, axis, pairs)  36 us
    ppermute x15, waiting for transfers between devices, shifted(): return lax.ppermute(value, axis, pairs)  13.7 us
    reshape x1, local copies, waits for them, and re-layouts, on_device(): image_grad.reshape(batch_here, angular_rows, views_here, rows_here, SCALE...  10.8 us
    reshape x1, local copies, waits for them, and re-layouts, on_device(): upscaled.transpose(0, 1, 2, 3, 4, 6, 5)  9.74 us
    dot_general x9, matrix products, epi_conv(): jnp.einsum('oc,buvhcw->buvhow', weight[tap_row, tap_col], padded[:, :, ta...  6.5 us
    all_to_all x1, waiting for transfers between devices, on_device(): lax.all_to_all(first_grad, 'ang', split_axis=2, concat_axis=3, tiled=True)  6.33 us
    dot_general x18, matrix products, weight_grad(): jnp.einsum('buvhow,buvhcw->oc', upstream, window, preferred_element_type=...  5.49 us
    dot_general x9, matrix products, spatial_conv(): jnp.einsum('oc,buvhcw->buvhow', weight[tap_row, tap_col], padded[:, :, :,...  5.47 us
  transfers between devices with their start and end apart: 21, of which 12 were waited for; matrix products, arithmetic and copies ran while one was open for 26% of the time, Pallas kernels for 0%

profile of v1, /device:TPU:1, one launch (start us, length us, event | category | flops | bytes accessed | tf_op | source)
XLA Modules:
  0.0 148.3 jit_solution(9038831059442655845)
XLA Ops:
  1.6 4.0 %collective-permute-start = (bf16[1,1,2,1,64,512]{5,4,3,2,1,0:T(8,128)(2,1)S(1)}, bf16[1,1,2,1,64,512]{5,4,3,2,1,0:T(8,128)(2,1)S(1)}, u32[]{:S(2)}, u32[]{:S(2)}) collective-permute-start(bf16[1,1,2,1,64,512]{5,4,3,2,1,0:T(8,128)(2,1)S(1)} %get-tuple-element.18), channel_id=1, source_target_pairs={{0,1},{1,2},{2,3},{3,4},{4,5},{5,6},{6,7},{7,8},{8,9},{9,10},{10,1... | collective-permute-start | bytes 393224 | tf_op jit(solution)/shard_map/ppermute | solution.py:18
  5.6 1.3 collective-permute-start.1
  6.9 10.8 %reshape.279 = bf16[1,1,2,4,4,512,4]{6,5,4,3,2,1,0:T(8,128)(2,1)} reshape(bf16[1,1,2,16,2048]{4,3,2,1,0:T(8,128)(2,1)} %param.9) | data formatting | bytes 262144 | tf_op jit(solution)/shard_map/reshape | solution.py:171
  17.7 3.8 %copy.164 = bf16[1,1,2,4,4,4,512]{6,3,5,4,2,1,0:T(4,128)(2,1)S(1)} copy(bf16[1,1,2,4,4,4,512]{5,6,4,3,2,1,0:T(8,128)(2,1)} %bitcast.482) | data formatting | bytes 262144 | tf_op jit(solution)/shard_map/transpose | solution.py:174
  26.6 1.5 %add_convert_fusion.1 = (bf16[1,1,2,4,64,512]{5,4,3,2,1,0:T(8,128)(2,1)S(1)}, f32[1,1,2,4,64,512]{5,4,3,2,1,0:T(8,128)}) fusion(bf16[1,1,2,4,64,512]{5,4,3,2,1,0:T(8,128)(2,1)S(1)} %copy-done.1, f32[2,4,512,64]{2,3,1,0:T(8,128)S(1)} %fusion.113, f32[2,4,512,64]{2,3,1,0:T(8,128)S(1)} %convolution_add_fusion.9, ...), kind=kOutput, calls=%fused_computation.81 | convolution fusion | flops 35913728 | bytes 4734976 | tf_op jit(solution)/shard_map/oc,buvhcw->buvhow/dot_general | solution.py:36
  29.0 4.2 %all-to-all-start = ((bf16[1,1,2,4,64,512]{5,4,2,1,0,3:T(8,128)(2,1)}), bf16[1,1,2,4,64,512]{5,4,2,1,0,3:T(8,128)(2,1)S(1)}, u32[]{:S(2)}, u32[]{:S(2)}) async-start(bf16[1,1,2,4,64,512]{5,4,2,1,0,3:T(8,128)(2,1)} %copy.160), calls=%async_computation | async-start | bytes 1048576 | tf_op jit(solution)/shard_map/all_to_all | solution.py:177
  34.0 2.3 %slice_bitcast_fusion.5 = (bf16[2,4,64,512]{3,2,1,0:T(8,128)(2,1)}, bf16[2,4,64,512]{3,2,1,0:T(8,128)(2,1)}, bf16[2,4,64,512]{3,2,1,0:T(8,128)(2,1)}, bf16[2,4,6...) fusion(bf16[1,1,2,6,64,514]{5,4,3,2,1,0:T(8,128)(2,1)S(1)} %fusion.15), kind=kLoop, calls=%fused_computation.111 | loop fusion | bytes 6291456 | tf_op jit(solution)/shard_map/reshape
  36.3 4.8 %all-to-all-done = bf16[1,1,2,4,64,512]{5,4,2,1,0,3:T(8,128)(2,1)S(1)} async-done(((bf16[1,1,2,4,64,512]{5,4,2,1,0,3:T(8,128)(2,1)}), bf16[1,1,2,4,64,512]{5,4,2,1,0,3:T(8,128)(2,1)S(1)}, u32[]{:S(2)}, u32[]{:S(2)}) %all-to-all-start) | async-done | bytes 524320 | tf_op jit(solution)/shard_map/all_to_all | solution.py:177
  41.1 3.6 %all-to-all-start.2 = ((bf16[4,1,1,2,1,64,512]{6,5,3,4,2,1,0:T(8,128)(2,1)}), bf16[4,1,1,2,1,64,512]{6,5,3,4,2,1,0:T(8,128)(2,1)S(1)}, u32[]{:S(2)}, u32[]{:S(2)}) async-start(bf16[4,1,1,2,1,64,512]{6,5,3,4,2,1,0:T(8,128)(2,1)} %pad_maximum_fusion.2), calls=%async_computation.2 | async-start | bytes 1048576 | tf_op jit(solution)/shard_map/all_to_all | solution.py:193
  48.5 3.0 %all-to-all-done.2 = bf16[4,1,1,2,1,64,512]{6,5,3,4,2,1,0:T(8,128)(2,1)S(1)} async-done(((bf16[4,1,1,2,1,64,512]{6,5,3,4,2,1,0:T(8,128)(2,1)}), bf16[4,1,1,2,1,64,512]{6,5,3,4,2,1,0:T(8,128)(2,1)S(1)}, u32[]{:S(2)}, u32[]{:S(2)}) %all-to-all-start.2) | async-done | bytes 524320 | tf_op jit(solution)/shard_map/all_to_all | solution.py:193
  51.5 2.9 %fusion.12 = (bf16[1,1,8,1,64,512]{5,4,2,3,1,0:T(8,128)(2,1)S(1)}, bf16[1,1,8,1,64,512]{5,4,3,1,0,2:T(8,128)(2,1)}) fusion(bf16[1,1,8,1,64,512]{5,4,2,3,1,0:T(8,128)(2,1)S(1)} %bitcast.485, bf16[1,1,8,1,64,512]{5,4,2,3,1,0:T(8,128)(2,1)S(1)} %bitcast.471, f32[8,512,64]{1,2,0:T(8,128)} %convolution_add_fusion.1, bf16[3,3,64,64]{3,2,1,0:T(8,128)(2,1)S(1)} %copy-done.3), kind=kOutput, calls=%fused_computation.76 | convolution fusion | flops 37486592 | bytes 3686400 | tf_op jit(solution)/shard_map/oc,buvhcw->buvhow/dot_general | solution.py:51
  61.6 3.5 %all-to-all-start.3 = ((bf16[1,1,8,1,64,512]{5,4,3,1,0,2:T(8,128)(2,1)}), bf16[1,1,8,1,64,512]{5,4,3,1,0,2:T(8,128)(2,1)S(1)}, u32[]{:S(2)}, u32[]{:S(2)}) async-start(bf16[1,1,8,1,64,512]{5,4,3,1,0,2:T(8,128)(2,1)} %fusion.7), calls=%async_computation.3 | async-start | bytes 1048576 | tf_op jit(solution)/shard_map/all_to_all | solution.py:201
  65.7 6.3 %all-to-all-done.3 = bf16[1,1,8,1,64,512]{5,4,3,1,0,2:T(8,128)(2,1)S(1)} async-done(((bf16[1,1,8,1,64,512]{5,4,3,1,0,2:T(8,128)(2,1)}), bf16[1,1,8,1,64,512]{5,4,3,1,0,2:T(8,128)(2,1)S(1)}, u32[]{:S(2)}, u32[]{:S(2)}) %all-to-all-start.3) | async-done | bytes 524320 | tf_op jit(solution)/shard_map/all_to_all | solution.py:201
  72.0 3.5 %all-to-all-start.1 = ((bf16[1,1,8,1,64,512]{5,4,3,1,0,2:T(8,128)(2,1)}), bf16[1,1,8,1,64,512]{5,4,3,1,0,2:T(8,128)(2,1)S(1)}, u32[]{:S(2)}, u32[]{:S(2)}) async-start(bf16[1,1,8,1,64,512]{5,4,3,1,0,2:T(8,128)(2,1)} %get-tuple-element.5), calls=%async_computation.1 | async-start | bytes 1048576 | tf_op jit(solution)/shard_map/all_to_all | solution.py:183
  79.2 3.2 %all-to-all-done.1 = bf16[1,1,8,1,64,512]{5,4,3,1,0,2:T(8,128)(2,1)S(1)} async-done(((bf16[1,1,8,1,64,512]{5,4,3,1,0,2:T(8,128)(2,1)}), bf16[1,1,8,1,64,512]{5,4,3,1,0,2:T(8,128)(2,1)S(1)}, u32[]{:S(2)}, u32[]{:S(2)}) %all-to-all-start.1) | async-done | bytes 524320 | tf_op jit(solution)/shard_map/all_to_all | solution.py:183
  82.8 1.8 %collective-permute-start.2 = (f32[152,128]{1,0:T(8,128)S(1)}, f32[152,128]{1,0:T(8,128)S(1)}, u32[]{:S(2)}, u32[]{:S(2)}) collective-permute-start(f32[152,128]{1,0:T(8,128)S(1)} %get-tuple-element.28), channel_id=1, source_target_pairs={{0,128},{64,192},{128,0},{192,64},{1,129},{65,193},{129,1},{193,65... | collective-permute-start | bytes 233480 | tf_op jit(solution)/shard_map/ppermute | solution.py:122
  84.5 5.9 %collective-permute-start.3 = (f32[152,128]{1,0:T(8,128)S(1)}, f32[152,128]{1,0:T(8,128)S(1)}, u32[]{:S(2)}, u32[]{:S(2)}) collective-permute-start(f32[152,128]{1,0:T(8,128)S(1)} %get-tuple-element.27), channel_id=1, source_target_pairs={{0,64},{64,128},{128,192},{192,0},{1,65},{65,129},{129,193},{193,1... | collective-permute-start | bytes 233480 | tf_op jit(solution)/shard_map/ppermute | solution.py:122
  90.7 1.5 %collective-permute-done.3 = f32[152,128]{1,0:T(8,128)S(1)} collective-permute-done((f32[152,128]{1,0:T(8,128)S(1)}, f32[152,128]{1,0:T(8,128)S(1)}, u32[]{:S(2)}, u32[]{:S(2)}) %collective-permute-start.3) | collective-permute-done | bytes 77856 | tf_op jit(solution)/shard_map/ppermute | solution.py:122
  92.2 2.5 %collective-permute-done.4 = f32[152,128]{1,0:T(8,128)S(1)} collective-permute-done((f32[152,128]{1,0:T(8,128)S(1)}, f32[152,128]{1,0:T(8,128)S(1)}, u32[]{:S(2)}, u32[]{:S(2)}) %collective-permute-start.4) | collective-permute-done | bytes 77856 | tf_op jit(solution)/shard_map/ppermute | solution.py:122
  94.7 3.7 %collective-permute-start.5 = (f32[152,128]{1,0:T(8,128)S(1)}, f32[152,128]{1,0:T(8,128)S(1)}, u32[]{:S(2)}, u32[]{:S(2)}) collective-permute-start(f32[152,128]{1,0:T(8,128)S(1)} %fusion.85), channel_id=1, source_target_pairs={{0,2},{1,3},{2,0},{3,1},{4,6},{5,7},{6,4},{7,5},{8,10},{9,11},{10,... | collective-permute-start | bytes 233480 | tf_op jit(solution)/shard_map/ppermute | solution.py:122
  98.3 1.8 %collective-permute-start.6 = (f32[152,128]{1,0:T(8,128)S(1)}, f32[152,128]{1,0:T(8,128)S(1)}, u32[]{:S(2)}, u32[]{:S(2)}) collective-permute-start(f32[152,128]{1,0:T(8,128)S(1)} %fusion.85), channel_id=1, source_target_pairs={{0,1},{1,2},{2,3},{3,0},{4,5},{5,6},{6,7},{7,4},{8,9},{9,10},{10,1... | collective-permute-start | bytes 233480 | tf_op jit(solution)/shard_map/ppermute | solution.py:122
  101.0 1.8 %collective-permute-done.6 = f32[152,128]{1,0:T(8,128)S(1)} collective-permute-done((f32[152,128]{1,0:T(8,128)S(1)}, f32[152,128]{1,0:T(8,128)S(1)}, u32[]{:S(2)}, u32[]{:S(2)}) %collective-permute-start.6) | collective-permute-done | bytes 77856 | tf_op jit(solution)/shard_map/ppermute | solution.py:122
  103.9 7.5 %collective-permute-start.10 = (f32[152,128]{1,0:T(8,128)S(1)}, f32[152,128]{1,0:T(8,128)S(1)}, u32[]{:S(2)}, u32[]{:S(2)}) collective-permute-start(f32[152,128]{1,0:T(8,128)S(1)} %add_add_fusion.2), channel_id=1, source_target_pairs={{0,12},{4,0},{8,4},{12,8},{1,13},{5,1},{9,5},{13,9},{2,14},{6,2},{... | collective-permute-start | bytes 233480 | tf_op jit(solution)/shard_map/ppermute | solution.py:122
  111.4 2.2 %collective-permute-start.8 = (f32[152,128]{1,0:T(8,128)S(1)}, f32[152,128]{1,0:T(8,128)S(1)}, u32[]{:S(2)}, u32[]{:S(2)}) collective-permute-start(f32[152,128]{1,0:T(8,128)S(1)} %add_add_fusion.2), channel_id=1, source_target_pairs={{0,8},{4,12},{8,0},{12,4},{1,9},{5,13},{9,1},{13,5},{2,10},{6,14},... | collective-permute-start | bytes 233480 | tf_op jit(solution)/shard_map/ppermute | solution.py:122
  113.6 2.3 %collective-permute-start.9 = (f32[152,128]{1,0:T(8,128)S(1)}, f32[152,128]{1,0:T(8,128)S(1)}, u32[]{:S(2)}, u32[]{:S(2)}) collective-permute-start(f32[152,128]{1,0:T(8,128)S(1)} %add_add_fusion.2), channel_id=1, source_target_pairs={{0,4},{4,8},{8,12},{12,0},{1,5},{5,9},{9,13},{13,1},{2,6},{6,10},{... | collective-permute-start | bytes 233480 | tf_op jit(solution)/shard_map/ppermute | solution.py:122
  115.9 2.8 %collective-permute-done.8 = f32[152,128]{1,0:T(8,128)S(1)} collective-permute-done((f32[152,128]{1,0:T(8,128)S(1)}, f32[152,128]{1,0:T(8,128)S(1)}, u32[]{:S(2)}, u32[]{:S(2)}) %collective-permute-start.8) | collective-permute-done | bytes 77856 | tf_op jit(solution)/shard_map/ppermute | solution.py:122
  118.7 1.5 collective-permute-done.9
  121.8 1.5 %collective-permute-start.13 = (f32[152,128]{1,0:T(8,128)S(1)}, f32[152,128]{1,0:T(8,128)S(1)}, u32[]{:S(2)}, u32[]{:S(2)}) collective-permute-start(f32[152,128]{1,0:T(8,128)S(1)} %add_add_fusion.1), channel_id=1, source_target_pairs={{0,48},{16,0},{32,16},{48,32},{1,49},{17,1},{33,17},{49,33},{2,50}... | collective-permute-start | bytes 233480 | tf_op jit(solution)/shard_map/ppermute | solution.py:122
  123.3 1.9 %collective-permute-done.11 = f32[152,128]{1,0:T(8,128)S(1)} collective-permute-done((f32[152,128]{1,0:T(8,128)S(1)}, f32[152,128]{1,0:T(8,128)S(1)}, u32[]{:S(2)}, u32[]{:S(2)}) %collective-permute-start.11) | collective-permute-done | bytes 77856 | tf_op jit(solution)/shard_map/ppermute | solution.py:122
  125.9 6.2 %collective-permute-start.14 = (f32[152,128]{1,0:T(8,128)S(1)}, f32[152,128]{1,0:T(8,128)S(1)}, u32[]{:S(2)}, u32[]{:S(2)}) collective-permute-start(f32[152,128]{1,0:T(8,128)S(1)} %add_add_fusion), channel_id=1, source_target_pairs={{0,64},{64,128},{128,192},{192,0},{1,65},{65,129},{129,193},{193,1... | collective-permute-start | bytes 233480 | tf_op jit(solution)/shard_map/ppermute | solution.py:122
  132.8 3.3 %copy.163 = bf16[1,1,2,4,4,4,512]{5,6,4,3,2,1,0:T(8,128)(2,1)} copy(bf16[1,1,2,4,4,4,512]{6,5,4,3,2,1,0:T(4,128)(2,1)S(1)} %reshape.277) | data formatting | bytes 262144 | tf_op jit(solution)/shard_map/reshape | solution.py:202
  136.1 9.7 %reshape.278 = bf16[1,1,2,16,2048]{4,3,2,1,0:T(8,128)(2,1)} reshape(bf16[1,1,2,4,4,512,4]{6,5,4,3,2,1,0:T(8,128)(2,1)} %bitcast.481) | data formatting | bytes 262144 | tf_op jit(solution)/shard_map/reshape | solution.py:205
  (120 shorter events, 30.7 us)
Async XLA Ops:
  0.6 20.9 %copy-start = (bf16[16,64]{1,0:T(8,128)(2,1)S(1)}, bf16[16,64]{1,0:T(8,128)(2,1)}, u32[]{:S(2)}) copy-start(bf16[16,64]{1,0:T(8,128)(2,1)} %param.8) | copy-start | bytes 6148
  1.6 20.3 %collective-permute-start = (bf16[1,1,2,1,64,512]{5,4,3,2,1,0:T(8,128)(2,1)S(1)}, bf16[1,1,2,1,64,512]{5,4,3,2,1,0:T(8,128)(2,1)S(1)}, u32[]{:S(2)}, u32[]{:S(2)}) collective-permute-start(bf16[1,1,2,1,64,512]{5,4,3,2,1,0:T(8,128)(2,1)S(1)} %get-tuple-element.18), channel_id=1, source_target_pairs={{0,1},{1,2},{2,3},{3,4},{4,5},{5,6},{6,7},{7,8},{8,9},{9,10},{10,1... | collective-permute-start | bytes 393224 | tf_op jit(solution)/shard_map/ppermute | solution.py:18
  5.6 16.3 %collective-permute-start.1 = (bf16[1,1,2,1,64,512]{5,4,3,2,1,0:T(8,128)(2,1)S(1)}, bf16[1,1,2,1,64,512]{5,4,3,2,1,0:T(8,128)(2,1)S(1)}, u32[]{:S(2)}, u32[]{:S(2)}) collective-permute-start(bf16[1,1,2,1,64,512]{5,4,3,2,1,0:T(8,128)(2,1)S(1)} %get-tuple-element.19), channel_id=1, source_target_pairs={{1,0},{2,1},{3,2},{4,3},{5,4},{6,5},{7,6},{8,7},{9,8},{10,9},{11,1... | collective-permute-start | bytes 393224 | tf_op jit(solution)/shard_map/ppermute | solution.py:20
  17.7 4.2 %copy-start.1 = (bf16[1,1,2,4,64,512]{5,4,3,2,1,0:T(8,128)(2,1)S(1)}, bf16[1,1,2,4,64,512]{5,4,3,2,1,0:T(8,128)(2,1)}, u32[]{:S(2)}) copy-start(bf16[1,1,2,4,64,512]{5,4,3,2,1,0:T(8,128)(2,1)} %param.5) | copy-start | bytes 1572868
  23.5 1.3 copy-start.12
  24.7 1.9 %copy-start.4 = (bf16[2,4,64,512]{3,2,1,0:T(8,128)(2,1)}, bf16[2,4,64,512]{3,2,1,0:T(8,128)(2,1)S(1)}, u32[]{:S(2)}) copy-start(bf16[2,4,64,512]{3,2,1,0:T(8,128)(2,1)S(1)} %get-tuple-element.16) | copy-start | bytes 1572868
  29.0 12.2 %all-to-all-start = ((bf16[1,1,2,4,64,512]{5,4,2,1,0,3:T(8,128)(2,1)}), bf16[1,1,2,4,64,512]{5,4,2,1,0,3:T(8,128)(2,1)S(1)}, u32[]{:S(2)}, u32[]{:S(2)}) async-start(bf16[1,1,2,4,64,512]{5,4,2,1,0,3:T(8,128)(2,1)} %copy.160), calls=%async_computation | async-start | bytes 1048576 | tf_op jit(solution)/shard_map/all_to_all | solution.py:177
  34.0 10.8 %copy-start.3 = (bf16[3,3,64,64]{3,2,1,0:T(8,128)(2,1)S(1)}, bf16[3,3,64,64]{3,2,1,0:T(8,128)(2,1)}, u32[]{:S(2)}) copy-start(bf16[3,3,64,64]{3,2,1,0:T(8,128)(2,1)} %param.7) | copy-start | bytes 221188
  41.1 10.4 %all-to-all-start.2 = ((bf16[4,1,1,2,1,64,512]{6,5,3,4,2,1,0:T(8,128)(2,1)}), bf16[4,1,1,2,1,64,512]{6,5,3,4,2,1,0:T(8,128)(2,1)S(1)}, u32[]{:S(2)}, u32[]{:S(2)}) async-start(bf16[4,1,1,2,1,64,512]{6,5,3,4,2,1,0:T(8,128)(2,1)} %pad_maximum_fusion.2), calls=%async_computation.2 | async-start | bytes 1048576 | tf_op jit(solution)/shard_map/all_to_all | solution.py:193
  61.6 10.4 %all-to-all-start.3 = ((bf16[1,1,8,1,64,512]{5,4,3,1,0,2:T(8,128)(2,1)}), bf16[1,1,8,1,64,512]{5,4,3,1,0,2:T(8,128)(2,1)S(1)}, u32[]{:S(2)}, u32[]{:S(2)}) async-start(bf16[1,1,8,1,64,512]{5,4,3,1,0,2:T(8,128)(2,1)} %fusion.7), calls=%async_computation.3 | async-start | bytes 1048576 | tf_op jit(solution)/shard_map/all_to_all | solution.py:201
  65.5 10.0 %copy-start.2 = (f32[1,1,2,4,64,512]{5,4,3,2,1,0:T(8,128)S(1)}, f32[1,1,2,4,64,512]{5,4,3,2,1,0:T(8,128)}, u32[]{:S(2)}) copy-start(f32[1,1,2,4,64,512]{5,4,3,2,1,0:T(8,128)} %get-tuple-element.30) | copy-start | bytes 3145732
  72.0 10.4 %all-to-all-start.1 = ((bf16[1,1,8,1,64,512]{5,4,3,1,0,2:T(8,128)(2,1)}), bf16[1,1,8,1,64,512]{5,4,3,1,0,2:T(8,128)(2,1)S(1)}, u32[]{:S(2)}, u32[]{:S(2)}) async-start(bf16[1,1,8,1,64,512]{5,4,3,1,0,2:T(8,128)(2,1)} %get-tuple-element.5), calls=%async_computation.1 | async-start | bytes 1048576 | tf_op jit(solution)/shard_map/all_to_all | solution.py:183
  76.2 1.1 copy-start.10
  76.5 1.1 copy-start.9
  77.0 1.1 copy-start.8
  77.3 1.1 copy-start.7
  77.6 1.1 copy-start.6
  82.8 7.9 %collective-permute-start.2 = (f32[152,128]{1,0:T(8,128)S(1)}, f32[152,128]{1,0:T(8,128)S(1)}, u32[]{:S(2)}, u32[]{:S(2)}) collective-permute-start(f32[152,128]{1,0:T(8,128)S(1)} %get-tuple-element.28), channel_id=1, source_target_pairs={{0,128},{64,192},{128,0},{192,64},{1,129},{65,193},{129,1},{193,65... | collective-permute-start | bytes 233480 | tf_op jit(solution)/shard_map/ppermute | solution.py:122
  84.5 7.6 %collective-permute-start.3 = (f32[152,128]{1,0:T(8,128)S(1)}, f32[152,128]{1,0:T(8,128)S(1)}, u32[]{:S(2)}, u32[]{:S(2)}) collective-permute-start(f32[152,128]{1,0:T(8,128)S(1)} %get-tuple-element.27), channel_id=1, source_target_pairs={{0,64},{64,128},{128,192},{192,0},{1,65},{65,129},{129,193},{193,1... | collective-permute-start | bytes 233480 | tf_op jit(solution)/shard_map/ppermute | solution.py:122
  90.4 4.3 %collective-permute-start.4 = (f32[152,128]{1,0:T(8,128)S(1)}, f32[152,128]{1,0:T(8,128)S(1)}, u32[]{:S(2)}, u32[]{:S(2)}) collective-permute-start(f32[152,128]{1,0:T(8,128)S(1)} %get-tuple-element.26), channel_id=1, source_target_pairs={{0,192},{64,0},{128,64},{192,128},{1,193},{65,1},{129,65},{193,129... | collective-permute-start | bytes 233480 | tf_op jit(solution)/shard_map/ppermute | solution.py:122
  94.7 6.4 %collective-permute-start.5 = (f32[152,128]{1,0:T(8,128)S(1)}, f32[152,128]{1,0:T(8,128)S(1)}, u32[]{:S(2)}, u32[]{:S(2)}) collective-permute-start(f32[152,128]{1,0:T(8,128)S(1)} %fusion.85), channel_id=1, source_target_pairs={{0,2},{1,3},{2,0},{3,1},{4,6},{5,7},{6,4},{7,5},{8,10},{9,11},{10,... | collective-permute-start | bytes 233480 | tf_op jit(solution)/shard_map/ppermute | solution.py:122
  98.3 4.5 %collective-permute-start.6 = (f32[152,128]{1,0:T(8,128)S(1)}, f32[152,128]{1,0:T(8,128)S(1)}, u32[]{:S(2)}, u32[]{:S(2)}) collective-permute-start(f32[152,128]{1,0:T(8,128)S(1)} %fusion.85), channel_id=1, source_target_pairs={{0,1},{1,2},{2,3},{3,0},{4,5},{5,6},{6,7},{7,4},{8,9},{9,10},{10,1... | collective-permute-start | bytes 233480 | tf_op jit(solution)/shard_map/ppermute | solution.py:122
  100.1 3.7 %collective-permute-start.7 = (f32[152,128]{1,0:T(8,128)S(1)}, f32[152,128]{1,0:T(8,128)S(1)}, u32[]{:S(2)}, u32[]{:S(2)}) collective-permute-start(f32[152,128]{1,0:T(8,128)S(1)} %fusion.85), channel_id=1, source_target_pairs={{0,3},{1,0},{2,1},{3,2},{4,7},{5,4},{6,5},{7,6},{8,11},{9,8},{10,9... | collective-permute-start | bytes 233480 | tf_op jit(solution)/shard_map/ppermute | solution.py:122
  103.9 12.0 %collective-permute-start.10 = (f32[152,128]{1,0:T(8,128)S(1)}, f32[152,128]{1,0:T(8,128)S(1)}, u32[]{:S(2)}, u32[]{:S(2)}) collective-permute-start(f32[152,128]{1,0:T(8,128)S(1)} %add_add_fusion.2), channel_id=1, source_target_pairs={{0,12},{4,0},{8,4},{12,8},{1,13},{5,1},{9,5},{13,9},{2,14},{6,2},{... | collective-permute-start | bytes 233480 | tf_op jit(solution)/shard_map/ppermute | solution.py:122
  111.4 7.3 %collective-permute-start.8 = (f32[152,128]{1,0:T(8,128)S(1)}, f32[152,128]{1,0:T(8,128)S(1)}, u32[]{:S(2)}, u32[]{:S(2)}) collective-permute-start(f32[152,128]{1,0:T(8,128)S(1)} %add_add_fusion.2), channel_id=1, source_target_pairs={{0,8},{4,12},{8,0},{12,4},{1,9},{5,13},{9,1},{13,5},{2,10},{6,14},... | collective-permute-start | bytes 233480 | tf_op jit(solution)/shard_map/ppermute | solution.py:122
  113.6 6.6 %collective-permute-start.9 = (f32[152,128]{1,0:T(8,128)S(1)}, f32[152,128]{1,0:T(8,128)S(1)}, u32[]{:S(2)}, u32[]{:S(2)}) collective-permute-start(f32[152,128]{1,0:T(8,128)S(1)} %add_add_fusion.2), channel_id=1, source_target_pairs={{0,4},{4,8},{8,12},{12,0},{1,5},{5,9},{9,13},{13,1},{2,6},{6,10},{... | collective-permute-start | bytes 233480 | tf_op jit(solution)/shard_map/ppermute | solution.py:122
  120.2 4.9 %collective-permute-start.11 = (f32[152,128]{1,0:T(8,128)S(1)}, f32[152,128]{1,0:T(8,128)S(1)}, u32[]{:S(2)}, u32[]{:S(2)}) collective-permute-start(f32[152,128]{1,0:T(8,128)S(1)} %add_add_fusion.1), channel_id=1, source_target_pairs={{0,32},{16,48},{32,0},{48,16},{1,33},{17,49},{33,1},{49,17},{2,34}... | collective-permute-start | bytes 233480 | tf_op jit(solution)/shard_map/ppermute | solution.py:122
  120.6 5.3 %collective-permute-start.12 = (f32[152,128]{1,0:T(8,128)S(1)}, f32[152,128]{1,0:T(8,128)S(1)}, u32[]{:S(2)}, u32[]{:S(2)}) collective-permute-start(f32[152,128]{1,0:T(8,128)S(1)} %add_add_fusion.1), channel_id=1, source_target_pairs={{0,16},{16,32},{32,48},{48,0},{1,17},{17,33},{33,49},{49,1},{2,18}... | collective-permute-start | bytes 233480 | tf_op jit(solution)/shard_map/ppermute | solution.py:122
  121.8 4.1 %collective-permute-start.13 = (f32[152,128]{1,0:T(8,128)S(1)}, f32[152,128]{1,0:T(8,128)S(1)}, u32[]{:S(2)}, u32[]{:S(2)}) collective-permute-start(f32[152,128]{1,0:T(8,128)S(1)} %add_add_fusion.1), channel_id=1, source_target_pairs={{0,48},{16,0},{32,16},{48,32},{1,49},{17,1},{33,17},{49,33},{2,50}... | collective-permute-start | bytes 233480 | tf_op jit(solution)/shard_map/ppermute | solution.py:122
  125.9 19.9 %collective-permute-start.14 = (f32[152,128]{1,0:T(8,128)S(1)}, f32[152,128]{1,0:T(8,128)S(1)}, u32[]{:S(2)}, u32[]{:S(2)}) collective-permute-start(f32[152,128]{1,0:T(8,128)S(1)} %add_add_fusion), channel_id=1, source_target_pairs={{0,64},{64,128},{128,192},{192,0},{1,65},{65,129},{129,193},{193,1... | collective-permute-start | bytes 233480 | tf_op jit(solution)/shard_map/ppermute | solution.py:122
  132.1 13.8 %collective-permute-start.15 = (f32[152,128]{1,0:T(8,128)S(1)}, f32[152,128]{1,0:T(8,128)S(1)}, u32[]{:S(2)}, u32[]{:S(2)}) collective-permute-start(f32[152,128]{1,0:T(8,128)S(1)} %add_add_fusion), channel_id=1, source_target_pairs={{0,128},{64,192},{128,0},{192,64},{1,129},{65,193},{129,1},{193,65... | collective-permute-start | bytes 233480 | tf_op jit(solution)/shard_map/ppermute | solution.py:122
  132.1 13.8 %collective-permute-start.16 = (f32[152,128]{1,0:T(8,128)S(1)}, f32[152,128]{1,0:T(8,128)S(1)}, u32[]{:S(2)}, u32[]{:S(2)}) collective-permute-start(f32[152,128]{1,0:T(8,128)S(1)} %add_add_fusion), channel_id=1, source_target_pairs={{0,192},{64,0},{128,64},{192,128},{1,193},{65,1},{129,65},{193,129... | collective-permute-start | bytes 233480 | tf_op jit(solution)/shard_map/ppermute | solution.py:122
  (2 other events, 2.1 us)
